TPU v7x, 256 devices: a whole 4x4x8 slice. The times are simulated.
256 devices in a mesh: rep: 64 (over x_lo, z, y), blk: 4 (over x_hi, core).
Axes of the slice: x: 4 (x_hi: 2, x_lo: 2; x = x_hi * 2 + x_lo), y: 4, z: 8, core: 2. Of those that a mesh axis runs over, the one named last changes fastest.
Arguments:
- encoded: bfloat16 [1024, 512, 512], P(('rep', 'blk')), may hold values from -6 to 6
- queries: bfloat16 [1024, 512], P('blk'), may hold values from -0.25 to 0.25
- classifiers: bfloat16 [1024, 512], P('blk'), may hold values from -1 to 1
- lengths: int32 [1024], P(('rep', 'blk')), may hold values from 1 to 512, 393216 in all
- beam: int32 [1024, 1024], P(('rep', 'blk')), may hold values 0 or 1
- logit_grad: float32 [1024, 1024], P(('rep', 'blk')), may hold values from -24 to 24
Outputs:
- logits: float32 [1024, 1024], P(('rep', 'blk'))
- encoded_grad: bfloat16 [1024, 512, 512], P(('rep', 'blk'))
- label_grad: float32 [1024, 1024], P('blk')
Inputs may be any that keep to these rules, and one draw needn't show every extreme that they name: `lengths`: every document has at least one real token, and some document has exactly 512.
All inputs are finite; a program needn't handle non-finite values. No bound on the sum of `lengths` or of `beam` on one device may be relied on, other than what follows from the above.
Results may differ from a plain program's by a relative error of at most 0.0058.
Values may be sent and summed in bfloat16 or wider, within the bound.
A program may use at most 64 MiB of HBM per device.

v0:
```python
import jax
import jax.numpy as jnp
from jax import lax
from jax.sharding import PartitionSpec as P


def one_document(states, length, beam_row, grad_row, queries, classifiers):
    scores = jnp.dot(queries, states.T, preferred_element_type=jnp.float32)
    valid = jnp.arange(states.shape[0]) < length
    expo = jnp.where(valid[None, :], jnp.exp(scores), 0.0)
    attn = expo / jnp.sum(expo, axis=1, keepdims=True)
    attn_b = attn.astype(jnp.bfloat16)
    context = jnp.dot(attn_b, states, preferred_element_type=jnp.float32)
    cls_f = classifiers.astype(jnp.float32)
    logit = jnp.sum(context * cls_f, axis=1)
    g_row = grad_row * beam_row.astype(jnp.float32)
    ctx_grad = (g_row[:, None] * cls_f).astype(jnp.bfloat16)
    attn_grad = jnp.dot(ctx_grad, states.T, preferred_element_type=jnp.float32)
    score_grad = (attn * (attn_grad - jnp.sum(attn * attn_grad, axis=1, keepdims=True))).astype(
        jnp.bfloat16
    )
    query_grad = jnp.dot(score_grad, states, preferred_element_type=jnp.float32)
    class_grad = g_row[:, None] * context
    state_grad = jnp.dot(attn_b.T, ctx_grad, preferred_element_type=jnp.float32) + jnp.dot(
        score_grad.T, queries, preferred_element_type=jnp.float32
    )
    return (logit, query_grad, class_grad, state_grad)


def per_device(encoded, queries, classifiers, lengths, beam, logit_grad):
    doc_count = encoded.shape[0]
    width = encoded.shape[2]
    query_piece = lax.all_gather(queries, "blk", axis=0, tiled=True)
    class_piece = lax.all_gather(classifiers, "blk", axis=0, tiled=True)
    count = query_piece.shape[0]
    term_piece = jnp.zeros((count, 2 * width), jnp.float32)
    logit_rows = []
    state_rows = []
    for doc in range(doc_count):
        beam_row = beam[doc]
        grad_row = logit_grad[doc]
        logit, query_grad, class_grad, state_grad = one_document(
            encoded[doc], lengths[doc], beam_row, grad_row, query_piece, class_piece
        )
        term_piece = term_piece + jnp.concatenate([query_grad, class_grad], axis=1)
        logit_rows.append(logit)
        state_rows.append(state_grad)
    logit_new = jnp.stack(logit_rows)
    state_new = jnp.stack(state_rows)
    shared = lax.psum_scatter(term_piece, "blk", scatter_dimension=0, tiled=True)
    label_grad = lax.psum(shared, "rep")
    return (logit_new, state_new.astype(jnp.bfloat16), label_grad)


def solution(mesh):
    in_specs = (
        P(("rep", "blk"), None, None),
        P("blk", None),
        P("blk", None),
        P(("rep", "blk")),
        P(("rep", "blk"), None),
        P(("rep", "blk"), None),
    )
    out_specs = (P(("rep", "blk"), None), P(("rep", "blk"), None, None), P("blk", None))
    return jax.shard_map(
        per_device, mesh=mesh, in_specs=in_specs, out_specs=out_specs, check_vma=False
    )
```

profile of v0, /device:TPU:2, one launch (start us, length us, event | category | flops | bytes accessed | tf_op | source)
XLA Modules:
  0.0 762.1 jit_solution(16452915523181712862)
XLA Ops:
  7.9 1.8 copy.9
  9.8 1.5 fusion.102
  13.9 1.0 convert_multiply_fusion.11
  14.8 20.3 %all-gather.3.cloned.1.call-done = bf16[1024,512]{1,0:T(8,128)(2,1)} async-done(((bf16[256,512]{1,0:T(8,128)(2,1)}), bf16[1024,512]{1,0:T(8,128)(2,1)}) %all-gather.3.cloned.1.call-update) | async-done | bytes 1048592 | tf_op jit(solution)/shard_map/all_gather | solution.py:33
  35.1 2.1 fusion.11
  37.3 23.1 %all-gather.5.cloned.1.call-done = bf16[1024,512]{0,1:T(8,128)(2,1)} async-done(((bf16[256,512]{0,1:T(8,128)(2,1)}), bf16[1024,512]{0,1:T(8,128)(2,1)}) %all-gather.5.cloned.1.call-update) | async-done | bytes 1048592 | tf_op jit(solution)/shard_map/all_gather | solution.py:34
  60.4 2.2 multiply_reduce_fusion.3
  63.2 1.0 copy-done.6
  66.3 0.9 fusion.59
  67.2 1.1 copy-done.12
  71.2 0.9 fusion.52
  75.1 0.9 fusion.45
  77.7 1.0 copy-done.4
  79.4 1.6 fusion.2
  81.0 3.7 fusion.1
  84.8 2.8 fusion.28
  87.6 1.5 fusion.22
  90.9 1.5 fusion.23
  93.7 1.5 fusion.24
  95.2 45.6 %reduce-scatter.2.cloned.1.call-done = f32[256,1024]{0,1:T(8,128)} async-done(((f32[1024,1024]{0,1:T(8,128)}), f32[256,1024]{0,1:T(8,128)}) %reduce-scatter.2.cloned.1.call-update) | async-done | bytes 1048592 | tf_op jit(solution)/shard_map/reduce_scatter | solution.py:50
  141.5 2.1 fusion.40
  144.9 1.6 pad_maximum_fusion
  146.5 606.6 %all-reduce.2.cloned.1.call-done = f32[256,1024]{0,1:T(8,128)} async-done(((f32[256,1024]{0,1:T(8,128)}), f32[256,1024]{0,1:T(8,128)}) %all-reduce.2.cloned.1.call-update) | async-done | bytes 1048592 | tf_op jit(solution)/shard_map/psum | solution.py:51
  753.1 2.5 copy.10
  (67 shorter events, 19.3 us)
Async XLA Ops:
  7.2 28.0 %all-gather.3.cloned.1.call-start = ((), (), s32[]{:S(2)}) async-start(), calls=%async_computation.1 | async-start | bytes 1310720 | tf_op jit(solution)/shard_map/all_gather | solution.py:33
  7.9 52.5 %all-gather.5.cloned.1.call-start = ((), (), s32[]{:S(2)}) async-start(), calls=%async_computation.2 | async-start | bytes 1310720 | tf_op jit(solution)/shard_map/all_gather | solution.py:34
  9.8 131.1 %reduce-scatter.2.cloned.1.call-start = ((), (), s32[]{:S(2)}) async-start(), calls=%async_computation.3 | async-start | bytes 5242880 | tf_op jit(solution)/shard_map/reduce_scatter | solution.py:50
  62.6 1.6 copy-start.6
  64.2 1.2 copy-start.17
  66.3 2.8 copy-start.7
  66.3 2.0 copy-start.12
  69.7 1.6 copy-start
  71.2 1.7 copy-start.9
  73.5 1.6 copy-start.2
  75.1 1.7 copy-start.11
  77.7 1.0 copy-start.4
  84.7 668.3 %all-reduce.2.cloned.1.call-start = ((), (), s32[]{:S(2)}) async-start(), calls=%async_computation.4 | async-start | bytes 2097152 | tf_op jit(solution)/shard_map/psum | solution.py:51
  84.8 2.8 copy-start.5
  84.8 2.8 copy-start.18
  87.6 1.6 copy-start.10
  87.6 2.0 copy-start.13
  89.6 1.2 copy-start.3
  90.9 1.6 copy-start.8
  92.5 1.2 copy-start.1
  141.5 2.1 copy-start.19
  143.6 1.0 copy-start.14
  143.6 1.2 copy-start.15
  143.6 1.3 copy-start.16
Sparse Core Ops, SparseCore 0:
  9.8 25.3 all-gather.2
  37.5 22.8 all-gather.4
  84.9 55.9 reduce-scatter.1
  143.3 609.7 all-reduce.1
where the time goes:
time: 763 us; the launch traced here: 762 us
  waiting for transfers between devices  696 us (91%)
  matrix products  28.1 us (4%)
  between operations  14.1 us (2%)
  other arithmetic  11.9 us (2%)
  local copies, waits for them, and re-layouts  11.5 us (2%)
    psum x1, waiting for transfers between devices, per_device(): label_grad = lax.psum(shared, 'rep')  607 us
    reduce_scatter x1, waiting for transfers between devices, per_device(): lax.psum_scatter(term_piece, 'blk', scatter_dimension=0, tiled=True)  45.6 us
    all_gather x1, waiting for transfers between devices, per_device(): class_piece = lax.all_gather(classifiers, 'blk', axis=0, tiled=True)  23.1 us
    all_gather x1, waiting for transfers between devices, per_device(): query_piece = lax.all_gather(queries, 'blk', axis=0, tiled=True)  20.3 us
  transfers between devices with their start and end apart: 4, of which 4 were waited for; matrix products, arithmetic and copies ran while one was open for 3% of the time, Pallas kernels for 0%

commit v1 on v0

v1 whole, which is shorter than its diff:
```python
import jax
import jax.numpy as jnp
from jax import lax
from jax.experimental import pallas as pl
from jax.experimental.pallas import tpu as pltpu
from jax.sharding import PartitionSpec as P

MESH = pl.DeviceIdType.MESH
F32 = jnp.float32
BF16 = jnp.bfloat16
E = 512
L = 512
DOCS = 4
T = DOCS * L
HB = 128
NEG = -1e30


def body(
    enc_hbm, q_hbm, c_hbm, len_ref, beam_ref, grad_ref,
    logit_ref, eg_ref, lg_ref,
    S, ST, W, GA, SP, G, acc, eacc,
    dsend, drecv, ysend, yrecv, yown, xsend, xrecv, xown, zsend, zrecv, zown, agp,
    lsem, gs, gr, ds, dr, ys, yr, xs, xr, zs, zr, as_, ar, ps, pr,
):
    rep = lax.axis_index("rep")
    blk = lax.axis_index("blk")
    x_lo = rep // 32
    z = (rep // 4) % 8
    y = rep % 4
    x_hi = blk // 2
    core = blk % 2

    def dev(xl, zz, yy, xh, cc):
        return ((xl * 8 + zz) * 4 + yy, xh * 2 + cc)

    partner = dev(x_lo, z, y, x_hi, 1 - core)
    across = dev(1 - x_lo, z, y, 1 - x_hi, core)
    across2 = dev(x_lo, z, y, 1 - x_hi, core)
    xpair = dev(1 - x_lo, z, y, x_hi, core)
    place = y * 2 + x_lo

    def ynb(k):
        return dev(x_lo, z, (y + k) % 4, x_hi, core)

    def znb(k):
        return dev(x_lo, (z + k) % 8, y, x_hi, core)

    def pnb(k):
        pp = (place + k) % 8
        return dev(pp % 2, z, pp // 2, x_hi, core)

    def local(src, dst, i):
        cp = pltpu.make_async_copy(src, dst, lsem.at[i])
        cp.start()
        return cp

    def remote(src, dst, ssem, rsem, to):
        return pltpu.make_async_remote_copy(
            src_ref=src, dst_ref=dst, send_sem=ssem, recv_sem=rsem,
            device_id=to, device_id_type=MESH,
        )

    pending = []

    def go(cp):
        cp.start()
        pending.append(cp)
        return cp

    weights = []
    for p in range(2):
        weights.append(local(q_hbm.at[pl.ds(p * HB, HB)], W.at[p, pl.ds(0, HB)], 2 * p))
        weights.append(local(c_hbm.at[pl.ds(p * HB, HB)], W.at[p, pl.ds(HB, HB)], 2 * p + 1))
    states = [local(enc_hbm.at[pl.ds(d * L, L)], S.at[pl.ds(d * L, L)], 4 + d) for d in range(DOCS)]

    barrier = pltpu.get_barrier_semaphore()
    greet = [partner, across, across2] + [znb(k) for k in range(1, 8)] + [pnb(k) for k in range(1, 8)]
    for to in greet:
        pl.semaphore_signal(barrier, inc=1, device_id=to, device_id_type=MESH)
    G[...] = grad_ref[...] * beam_ref[...].astype(F32)
    for cp in weights:
        cp.wait()
    pl.semaphore_wait(barrier, len(greet))

    to_partner = [go(remote(W.at[p], W.at[2 + p], gs.at[p], gr.at[p], partner)) for p in range(2)]
    to_across = [go(remote(W.at[p], W.at[5 + 2 * p], gs.at[2 + p], gr.at[2 + p], across)) for p in range(2)]
    to_fwd = [remote(W.at[5 + 2 * p], W.at[4 + 2 * p], gs.at[4 + p], gr.at[4 + p], partner) for p in range(2)]

    for d in range(DOCS):
        states[d].wait()
        ST[:, pl.ds(d * L, L)] = S[pl.ds(d * L, L), :].T

    own0 = blk * 256
    par0 = (x_hi * 2 + 1 - core) * 256
    far_own0 = ((1 - x_hi) * 2 + core) * 256
    far_par0 = ((1 - x_hi) * 2 + 1 - core) * 256
    starts = [own0, own0 + HB, par0, par0 + HB, far_par0, far_own0, far_par0 + HB, far_own0 + HB]

    row = lax.broadcasted_iota(jnp.int32, (L, HB), 0)

    def slot(k):
        at = pl.ds(pl.multiple_of(starts[k], HB), HB)
        w = W[k]
        for d in range(DOCS):
            SP[pl.ds(d * L, L), :] = lax.dot_general(
                S[pl.ds(d * L, L), :], w, (((1,), (1,)), ((), ())), preferred_element_type=F32
            )
        for d in range(DOCS):
            rows = pl.ds(d * L, L)
            sc = jnp.where(row < len_ref[d], SP[rows, pl.ds(0, HB)], NEG)
            pr_ = SP[rows, pl.ds(HB, HB)]
            ex = jnp.exp(sc - jnp.max(sc, axis=0, keepdims=True))
            inv = 1.0 / jnp.sum(ex, axis=0, keepdims=True)
            lg = jnp.sum(ex * pr_, axis=0, keepdims=True) * inv
            logit_ref[pl.ds(d, 1), at] = lg
            ag = ex * (inv * G[pl.ds(d, 1), at])
            GA[rows, pl.ds(k * 256 + HB, HB)] = ag.astype(BF16)
            GA[rows, pl.ds(k * 256, HB)] = (ag * (pr_ - lg)).astype(BF16)
        return jnp.dot(ST[...], GA[:, pl.ds(k * 256, 256)], preferred_element_type=F32)

    def state_grad(first):
        def tile(i, carry):
            rows = pl.ds(pl.multiple_of(i * 256, 256), 256)
            if first:
                eacc[rows, :] = jnp.dot(
                    GA[rows, pl.ds(0, 1024)], W[pl.ds(0, 4)].reshape(1024, E), preferred_element_type=F32
                )
            else:
                eg_ref[rows, :] = (
                    eacc[rows, :]
                    + jnp.dot(
                        GA[rows, pl.ds(1024, 1024)], W[pl.ds(4, 4)].reshape(1024, E), preferred_element_type=F32
                    )
                ).astype(BF16)
            return carry

        return tile

    def die_send(j, value):
        dsend[j] = value.astype(BF16)
        return go(remote(dsend.at[j], drecv.at[j], ds.at[j], dr.at[j], partner))

    def y_send(j, dcp, own):
        dcp.wait_recv()
        total = own + drecv[j].astype(F32)
        yown[j] = total.reshape(4, 128, 256)
        ysend[j] = total.astype(BF16).reshape(4, 128, 256)
        return [
            go(remote(ysend.at[j, (y + k) % 4], yrecv.at[j, k - 1], ys.at[j, k - 1], yr.at[j, k - 1], ynb(k)))
            for k in range(1, 4)
        ]

    def y_sum(j, cps):
        for cp in cps:
            cp.wait_recv()
        total = yown[j, y]
        for k in range(3):
            total = total + yrecv[j, k].astype(F32)
        return total

    def x_send_home(p, cps):
        total = y_sum(p, cps).reshape(2, 64, 256)
        xown[p] = total
        xsend[p] = total.astype(BF16)
        return go(remote(xsend.at[p, 1 - x_lo], xrecv.at[p, 0], xs.at[p, 0], xr.at[p, 0], xpair))

    def x_send_away(p, cps):
        total = y_sum(2 + p, cps).reshape(2, 64, 256)
        xsend[2 + p] = total.astype(BF16)
        return [
            go(remote(xsend.at[2 + p, x_lo], xrecv.at[p, 1], xs.at[p, 1], xr.at[p, 1], across2)),
            go(remote(xsend.at[2 + p, 1 - x_lo], xrecv.at[p, 2], xs.at[p, 2], xr.at[p, 2], across)),
        ]

    def z_send(p, cps):
        for cp in cps:
            cp.wait_recv()
        total = xown[p, x_lo]
        for k in range(3):
            total = total + xrecv[p, k].astype(F32)
        for i in range(4):
            for j in range(2):
                piece = total[i * 16 : (i + 1) * 16, j * 128 : (j + 1) * 128]
                zown[p, i * 2 + j] = piece
                zsend[p, i * 2 + j] = piece.astype(BF16)
        return [
            go(remote(zsend.at[p, (z + k) % 8], zrecv.at[p, k - 1], zs.at[p, k - 1], zr.at[p, k - 1], znb(k)))
            for k in range(1, 8)
        ]

    def az_send(p, cps):
        for cp in cps:
            cp.wait_recv()
        total = zown[p, z]
        for k in range(7):
            total = total + zrecv[p, k].astype(F32)
        agp[p, place, z] = total.astype(BF16)
        return [
            go(remote(agp.at[p, place, z], agp.at[p, place, z], as_.at[p, k - 1], ar.at[p, k - 1], znb(k)))
            for k in range(1, 8)
        ]

    def ap_send(p, cps):
        for cp in cps:
            cp.wait_recv()
        return [
            go(remote(agp.at[p, place], agp.at[p, place], ps.at[p, k - 1], pr.at[p, k - 1], pnb(k)))
            for k in range(1, 8)
        ]

    def finish(p, cps):
        for cp in cps:
            cp.wait_recv()
        for j in range(2):
            parts = [agp[p, a, i * 2 + j] for a in range(8) for i in range(4)]
            whole = jnp.concatenate(parts, axis=0).astype(F32)
            lg_ref[pl.ds(p * HB, HB), pl.ds(j * E, E)] = whole.T

    acc[0] = slot(0)
    acc[1] = slot(1)
    to_partner[0].wait_recv()
    d0 = die_send(0, slot(2))
    to_partner[1].wait_recv()
    d1 = die_send(1, slot(3))
    y0 = y_send(0, d0, acc[0])
    to_across[0].wait_recv()
    go(to_fwd[0])
    y1 = y_send(1, d1, acc[1])
    lax.fori_loop(0, 8, state_grad(True), 0)
    xa0 = x_send_home(0, y0)
    xa1 = x_send_home(1, y1)
    to_fwd[0].wait_recv()
    d2 = die_send(2, slot(4))
    y2 = y_send(2, d2, slot(5))
    to_across[1].wait_recv()
    go(to_fwd[1])
    to_fwd[1].wait_recv()
    d3 = die_send(3, slot(6))
    xb0 = x_send_away(0, y2)
    y3 = y_send(3, d3, slot(7))
    z0 = z_send(0, [xa0] + xb0)
    lax.fori_loop(0, 3, state_grad(False), 0)
    xb1 = x_send_away(1, y3)
    lax.fori_loop(3, 5, state_grad(False), 0)
    az0 = az_send(0, z0)
    z1 = z_send(1, [xa1] + xb1)
    lax.fori_loop(5, 8, state_grad(False), 0)
    ap0 = ap_send(0, az0)
    az1 = az_send(1, z1)
    ap1 = ap_send(1, az1)
    finish(0, ap0)
    finish(1, ap1)
    for cp in pending:
        cp.wait_send()


def per_device(encoded, queries, classifiers, lengths, beam, logit_grad):
    any_spec = pl.BlockSpec(memory_space=pl.ANY)
    vm = pl.BlockSpec(memory_space=pltpu.VMEM)
    dma = pltpu.SemaphoreType.DMA
    logits, eg, lg = pl.pallas_call(
        body,
        out_shape=(
            jax.ShapeDtypeStruct((DOCS, 1024), F32),
            jax.ShapeDtypeStruct((T, E), BF16),
            jax.ShapeDtypeStruct((256, 1024), F32),
        ),
        in_specs=[any_spec, any_spec, any_spec, pl.BlockSpec(memory_space=pltpu.SMEM), vm, vm],
        out_specs=(vm, vm, vm),
        scratch_shapes=[
            pltpu.VMEM((T, E), BF16),
            pltpu.VMEM((E, T), BF16),
            pltpu.VMEM((8, 256, E), BF16),
            pltpu.VMEM((T, 2048), BF16),
            pltpu.VMEM((T, 256), F32),
            pltpu.VMEM((DOCS, 1024), F32),
            pltpu.VMEM((2, E, 256), F32),
            pltpu.VMEM((T, E), F32),
            pltpu.VMEM((4, E, 256), BF16),
            pltpu.VMEM((4, E, 256), BF16),
            pltpu.VMEM((4, 4, 128, 256), BF16),
            pltpu.VMEM((4, 3, 128, 256), BF16),
            pltpu.VMEM((4, 4, 128, 256), F32),
            pltpu.VMEM((4, 2, 64, 256), BF16),
            pltpu.VMEM((2, 3, 64, 256), BF16),
            pltpu.VMEM((2, 2, 64, 256), F32),
            pltpu.VMEM((2, 8, 16, 128), BF16),
            pltpu.VMEM((2, 7, 16, 128), BF16),
            pltpu.VMEM((2, 8, 16, 128), F32),
            pltpu.VMEM((2, 8, 8, 16, 128), BF16),
            dma((8,)),
            dma((6,)), dma((6,)),
            dma((4,)), dma((4,)),
            dma((4, 3)), dma((4, 3)),
            dma((2, 3)), dma((2, 3)),
            dma((2, 7)), dma((2, 7)),
            dma((2, 7)), dma((2, 7)),
            dma((2, 7)), dma((2, 7)),
        ],
        compiler_params=pltpu.CompilerParams(
            collective_id=0, has_side_effects=True, vmem_limit_bytes=60 * 1024 * 1024
        ),
        name="attn",
    )(encoded.reshape(T, E), queries, classifiers, lengths, beam, logit_grad)
    return logits, eg.reshape(DOCS, L, E), lg


def solution(mesh):
    in_specs = (
        P(("rep", "blk"), None, None),
        P("blk", None),
        P("blk", None),
        P(("rep", "blk")),
        P(("rep", "blk"), None),
        P(("rep", "blk"), None),
    )
    out_specs = (P(("rep", "blk"), None), P(("rep", "blk"), None, None), P("blk", None))
    return jax.shard_map(
        per_device, mesh=mesh, in_specs=in_specs, out_specs=out_specs, check_vma=False
    )
```

time: 763 us -> 71.3 us (0.09)
  waiting for transfers between devices: 696 us -> 0 us
  Pallas kernels: 0 us -> 65 us
  matrix products: 28.1 us -> 0 us
  between operations: 14.1 us -> 0.64 us
  other arithmetic: 11.9 us -> 0 us
    psum x1 -> x0, waiting for transfers between devices: 607 us -> none  [per_device(): label_grad = lax.psum(shared, 'rep')]
    pallas_call x0 -> x1, Pallas kernels: none -> 65 us  [per_device(): pl.pallas_call(body, out_shape=(jax.ShapeDtypeStruct((DOCS, 1024), F32),...]
    reduce_scatter x1 -> x0, waiting for transfers between devices: 45.6 us -> none  [per_device(): lax.psum_scatter(term_piece, 'blk', scatter_dimension=0, tiled=True)]
    all_gather x2 -> x0, waiting for transfers between devices: 43.4 us -> none  [the longest x1 23.1 us: per_device(): class_piece = lax.all_gather(classifiers, 'blk', axis=0, tiled=True)]
    dot_general x24 -> x0, matrix products: 28.1 us -> none  [the longest x4 6.35 us: one_document(): jnp.dot(attn_b.T, ctx_grad, preferred_element_type=jnp.float32)]
  transfers between devices with their start and end apart: 4 -> 0, of which waited for: 4 -> 0; matrix products, arithmetic and copies ran while one was open for 3% -> 0% of each run, Pallas kernels for 0% -> 0%
where the time goes in v1:
time: 71.3 us; the launch traced here: 71 us
  Pallas kernels  65 us (91%)
  local copies, waits for them, and re-layouts  5.43 us (8%)
    pallas_call x1, Pallas kernels, per_device(): pl.pallas_call(body, out_shape=(jax.ShapeDtypeStruct((DOCS, 1024), F32),...  65 us
    unnamed x5, local copies, waits for them, and re-layouts  5.43 us

profile of v1, /device:TPU:2, one launch (start us, length us, event | category | flops | bytes accessed | tf_op | source)
XLA Modules:
  0.0 71.0 jit_solution(13015319606071997155)
XLA Ops:
  0.6 65.0 %attn.1 = (f32[4,1024]{1,0:T(4,128)}, bf16[2048,512]{1,0:T(8,128)(2,1)}, f32[256,1024]{1,0:T(8,128)}) custom-call(bf16[2048,512]{1,0:T(8,128)(2,1)} %bitcast.2, bf16[256,512]{1,0:T(8,128)(2,1)} %q_hbm.1, bf16[256,512]{1,0:T(8,128)(2,1)} %c_hbm.1, s32[4]{0:T(128)} %len_ref.1, s32[4,1024]{1,0:T(4,128)} %beam_ref.1, f32[4,1024]{1,0:T(4,128)} %grad_ref.1), custom_call_target="tpu_custom_call" | custom-call | tf_op jit(solution)/shard_map/attn/pallas_call | solution.py:262
  65.6 1.3 %copy.12 = f32[4,1024]{1,0:T(4,128)} copy(f32[4,1024]{1,0:T(4,128)} %get-tuple-element.12) | data formatting | bytes 32768
  66.9 0.0 copy-start
  66.9 3.1 %copy.13 = bf16[4,512,512]{2,1,0:T(8,128)(2,1)} copy(bf16[4,512,512]{2,1,0:T(8,128)(2,1)} %bitcast.3) | data formatting | bytes 4194304
  70.1 0.0 copy-done
  70.1 1.0 %copy.14 = f32[256,1024]{1,0:T(8,128)} copy(f32[256,1024]{1,0:T(8,128)S(1)} %copy-done) | data formatting | bytes 2097152
Async XLA Ops:
  66.9 3.1 %copy-start = (f32[256,1024]{1,0:T(8,128)S(1)}, f32[256,1024]{1,0:T(8,128)}, u32[]{:S(2)}) copy-start(f32[256,1024]{1,0:T(8,128)} %get-tuple-element.14) | copy-start | bytes 3145732

commit v2 on v1

--- a/solution.py
+++ b/solution.py
@@ -17,9 +17,9 @@
 
 
 def body(
-    enc_hbm, q_hbm, c_hbm, len_ref, beam_ref, grad_ref,
+    enc_hbm, q_hbm, c_hbm, len_hbm, beam_hbm, grad_hbm,
     logit_ref, eg_ref, lg_ref,
-    S, ST, W, GA, SP, G, acc, eacc,
+    S, ST, W, GA, SP, len_ref, beam_ref, grad_ref, G, acc, eacc,
     dsend, drecv, ysend, yrecv, yown, xsend, xrecv, xown, zsend, zrecv, zown, agp,
     lsem, gs, gr, ds, dr, ys, yr, xs, xr, zs, zr, as_, ar, ps, pr,
 ):
@@ -74,19 +74,28 @@
         weights.append(local(c_hbm.at[pl.ds(p * HB, HB)], W.at[p, pl.ds(HB, HB)], 2 * p + 1))
     states = [local(enc_hbm.at[pl.ds(d * L, L)], S.at[pl.ds(d * L, L)], 4 + d) for d in range(DOCS)]
 
+    small = [local(beam_hbm, beam_ref, 8), local(grad_hbm, grad_ref, 9), local(len_hbm, len_ref, 10)]
+
     barrier = pltpu.get_barrier_semaphore()
     greet = [partner, across, across2] + [znb(k) for k in range(1, 8)] + [pnb(k) for k in range(1, 8)]
     for to in greet:
         pl.semaphore_signal(barrier, inc=1, device_id=to, device_id_type=MESH)
-    G[...] = grad_ref[...] * beam_ref[...].astype(F32)
     for cp in weights:
         cp.wait()
     pl.semaphore_wait(barrier, len(greet))
 
     to_partner = [go(remote(W.at[p], W.at[2 + p], gs.at[p], gr.at[p], partner)) for p in range(2)]
-    to_across = [go(remote(W.at[p], W.at[5 + 2 * p], gs.at[2 + p], gr.at[2 + p], across)) for p in range(2)]
+    quarter = pl.ds(pl.multiple_of(y * 64, 64), 64)
+    to_across1 = go(remote(W.at[1, quarter], W.at[7, quarter], gs.at[2], gr.at[2], across))
+    to_across0 = go(remote(W.at[0], W.at[5], gs.at[3], gr.at[3], across))
+    to_ring = [
+        remote(W.at[7, quarter], W.at[7, quarter], gs.at[5 + k], gr.at[5 + k], ynb(k)) for k in range(1, 4)
+    ]
     to_fwd = [remote(W.at[5 + 2 * p], W.at[4 + 2 * p], gs.at[4 + p], gr.at[4 + p], partner) for p in range(2)]
 
+    for cp in small:
+        cp.wait()
+    G[...] = grad_ref[...] * beam_ref[...].astype(F32)
     for d in range(DOCS):
         states[d].wait()
         ST[:, pl.ds(d * L, L)] = S[pl.ds(d * L, L), :].T
@@ -99,25 +108,44 @@
 
     row = lax.broadcasted_iota(jnp.int32, (L, HB), 0)
 
-    def slot(k):
-        at = pl.ds(pl.multiple_of(starts[k], HB), HB)
-        w = W[k]
-        for d in range(DOCS):
+    def pair(k):
+        ats = [pl.ds(pl.multiple_of(starts[k + i], HB), HB) for i in range(2)]
+        w = W[pl.ds(k, 2)].reshape(512, E)
+        g = [[G[pl.ds(d, 1), at] for at in ats] for d in range(DOCS)]
+
+        def scores(d):
             SP[pl.ds(d * L, L), :] = lax.dot_general(
                 S[pl.ds(d * L, L), :], w, (((1,), (1,)), ((), ())), preferred_element_type=F32
             )
-        for d in range(DOCS):
+
+        def soft(d):
             rows = pl.ds(d * L, L)
-            sc = jnp.where(row < len_ref[d], SP[rows, pl.ds(0, HB)], NEG)
-            pr_ = SP[rows, pl.ds(HB, HB)]
-            ex = jnp.exp(sc - jnp.max(sc, axis=0, keepdims=True))
-            inv = 1.0 / jnp.sum(ex, axis=0, keepdims=True)
-            lg = jnp.sum(ex * pr_, axis=0, keepdims=True) * inv
-            logit_ref[pl.ds(d, 1), at] = lg
-            ag = ex * (inv * G[pl.ds(d, 1), at])
-            GA[rows, pl.ds(k * 256 + HB, HB)] = ag.astype(BF16)
-            GA[rows, pl.ds(k * 256, HB)] = (ag * (pr_ - lg)).astype(BF16)
-        return jnp.dot(ST[...], GA[:, pl.ds(k * 256, 256)], preferred_element_type=F32)
+            valid = row < len_ref[d]
+            for i in range(2):
+                sc = jnp.where(valid, SP[rows, pl.ds(i * 256, HB)], NEG)
+                pr_ = SP[rows, pl.ds(i * 256 + HB, HB)]
+                ex = jnp.exp(sc - jnp.max(sc, axis=0, keepdims=True))
+                inv = 1.0 / jnp.sum(ex, axis=0, keepdims=True)
+                lg = jnp.sum(ex * pr_, axis=0, keepdims=True) * inv
+                logit_ref[pl.ds(d, 1), ats[i]] = lg
+                ag = ex * (inv * g[d][i])
+                GA[rows, pl.ds((k + i) * 256 + HB, HB)] = ag.astype(BF16)
+                GA[rows, pl.ds((k + i) * 256, HB)] = (ag * (pr_ - lg)).astype(BF16)
+
+        def lab(d):
+            rows = pl.ds(d * L, 2 * L)
+            return jnp.dot(ST[:, rows], GA[rows, pl.ds(k * 256, 512)], preferred_element_type=F32)
+
+        scores(0)
+        scores(1)
+        soft(0)
+        scores(2)
+        soft(1)
+        out = lab(0)
+        scores(3)
+        soft(2)
+        soft(3)
+        return out + lab(2)
 
     def state_grad(first):
         def tile(i, carry):
@@ -217,35 +245,45 @@
             whole = jnp.concatenate(parts, axis=0).astype(F32)
             lg_ref[pl.ds(p * HB, HB), pl.ds(j * E, E)] = whole.T
 
-    acc[0] = slot(0)
-    acc[1] = slot(1)
-    to_partner[0].wait_recv()
-    d0 = die_send(0, slot(2))
-    to_partner[1].wait_recv()
-    d1 = die_send(1, slot(3))
+    out = pair(0)
+    acc[0] = out[:, :256]
+    acc[1] = out[:, 256:]
+    to_across1.wait_recv()
+    for cp in to_ring:
+        go(cp)
+    for cp in to_partner:
+        cp.wait_recv()
+    out = pair(2)
+    d0 = die_send(0, out[:, :256])
+    d1 = die_send(1, out[:, 256:])
+    lax.fori_loop(0, 4, state_grad(True), 0)
     y0 = y_send(0, d0, acc[0])
-    to_across[0].wait_recv()
+    lax.fori_loop(4, 8, state_grad(True), 0)
+    to_across0.wait_recv()
     go(to_fwd[0])
+    for cp in to_ring:
+        cp.wait_recv()
+    go(to_fwd[1])
     y1 = y_send(1, d1, acc[1])
-    lax.fori_loop(0, 8, state_grad(True), 0)
+    to_fwd[0].wait_recv()
+    out = pair(4)
+    d2 = die_send(2, out[:, :256])
+    acc[2] = out[:, 256:]
+    to_fwd[1].wait_recv()
+    y2 = y_send(2, d2, acc[2])
+    out = pair(6)
+    d3 = die_send(3, out[:, :256])
+    acc[3] = out[:, 256:]
     xa0 = x_send_home(0, y0)
+    y3 = y_send(3, d3, acc[3])
     xa1 = x_send_home(1, y1)
-    to_fwd[0].wait_recv()
-    d2 = die_send(2, slot(4))
-    y2 = y_send(2, d2, slot(5))
-    to_across[1].wait_recv()
-    go(to_fwd[1])
-    to_fwd[1].wait_recv()
-    d3 = die_send(3, slot(6))
     xb0 = x_send_away(0, y2)
-    y3 = y_send(3, d3, slot(7))
+    lax.fori_loop(0, 6, state_grad(False), 0)
     z0 = z_send(0, [xa0] + xb0)
-    lax.fori_loop(0, 3, state_grad(False), 0)
     xb1 = x_send_away(1, y3)
-    lax.fori_loop(3, 5, state_grad(False), 0)
+    lax.fori_loop(6, 8, state_grad(False), 0)
     az0 = az_send(0, z0)
     z1 = z_send(1, [xa1] + xb1)
-    lax.fori_loop(5, 8, state_grad(False), 0)
     ap0 = ap_send(0, az0)
     az1 = az_send(1, z1)
     ap1 = ap_send(1, az1)
@@ -255,8 +293,16 @@
         cp.wait_send()
 
 
+def writer(a, b, c, oa, ob, oc, sem):
+    copies = [pltpu.make_async_copy(src, dst, sem.at[i]) for i, (src, dst) in enumerate(((b, ob), (c, oc), (a, oa)))]
+    for cp in copies:
+        cp.start()
+    for cp in copies:
+        cp.wait()
+
+
 def per_device(encoded, queries, classifiers, lengths, beam, logit_grad):
-    any_spec = pl.BlockSpec(memory_space=pl.ANY)
+    hbm = pl.BlockSpec(memory_space=pltpu.HBM)
     vm = pl.BlockSpec(memory_space=pltpu.VMEM)
     dma = pltpu.SemaphoreType.DMA
     logits, eg, lg = pl.pallas_call(
@@ -266,16 +312,19 @@
             jax.ShapeDtypeStruct((T, E), BF16),
             jax.ShapeDtypeStruct((256, 1024), F32),
         ),
-        in_specs=[any_spec, any_spec, any_spec, pl.BlockSpec(memory_space=pltpu.SMEM), vm, vm],
+        in_specs=[hbm] * 6,
         out_specs=(vm, vm, vm),
         scratch_shapes=[
             pltpu.VMEM((T, E), BF16),
             pltpu.VMEM((E, T), BF16),
             pltpu.VMEM((8, 256, E), BF16),
             pltpu.VMEM((T, 2048), BF16),
-            pltpu.VMEM((T, 256), F32),
+            pltpu.VMEM((T, 512), F32),
+            pltpu.SMEM((DOCS,), jnp.int32),
+            pltpu.VMEM((DOCS, 1024), jnp.int32),
             pltpu.VMEM((DOCS, 1024), F32),
-            pltpu.VMEM((2, E, 256), F32),
+            pltpu.VMEM((DOCS, 1024), F32),
+            pltpu.VMEM((4, E, 256), F32),
             pltpu.VMEM((T, E), F32),
             pltpu.VMEM((4, E, 256), BF16),
             pltpu.VMEM((4, E, 256), BF16),
@@ -289,8 +338,8 @@
             pltpu.VMEM((2, 7, 16, 128), BF16),
             pltpu.VMEM((2, 8, 16, 128), F32),
             pltpu.VMEM((2, 8, 8, 16, 128), BF16),
-            dma((8,)),
-            dma((6,)), dma((6,)),
+            dma((11,)),
+            dma((9,)), dma((9,)),
             dma((4,)), dma((4,)),
             dma((4, 3)), dma((4, 3)),
             dma((2, 3)), dma((2, 3)),
@@ -299,10 +348,26 @@
             dma((2, 7)), dma((2, 7)),
         ],
         compiler_params=pltpu.CompilerParams(
-            collective_id=0, has_side_effects=True, vmem_limit_bytes=60 * 1024 * 1024
+            collective_id=0, has_side_effects=True, vmem_limit_bytes=46 * 1024 * 1024
         ),
         name="attn",
-    )(encoded.reshape(T, E), queries, classifiers, lengths, beam, logit_grad)
+    )(*[
+        pltpu.with_memory_space_constraint(v, pltpu.HBM)
+        for v in (encoded.reshape(T, E), queries, classifiers, lengths, beam, logit_grad)
+    ])
+    logits, eg, lg = pl.pallas_call(
+        writer,
+        out_shape=(
+            jax.ShapeDtypeStruct((DOCS, 1024), F32),
+            jax.ShapeDtypeStruct((T, E), BF16),
+            jax.ShapeDtypeStruct((256, 1024), F32),
+        ),
+        in_specs=[pl.BlockSpec(memory_space=pl.ANY)] * 3,
+        out_specs=(hbm, hbm, hbm),
+        scratch_shapes=[dma((3,))],
+        compiler_params=pltpu.CompilerParams(vmem_limit_bytes=4 * 1024 * 1024),
+        name="writer",
+    )(logits, eg, lg)
     return logits, eg.reshape(DOCS, L, E), lg
 
 

time: 71.3 us -> 57.7 us (0.81)
  Pallas kernels: 65 us -> 56.8 us
  local copies, waits for them, and re-layouts: 5.43 us -> 0 us
    pallas_call x1, Pallas kernels: 65 us -> 55.1 us  [per_device(): pl.pallas_call(body, out_shape=(jax.ShapeDtypeStruct((DOCS, 1024), F32),...]
    unnamed x5 -> x0, local copies, waits for them, and re-layouts: 5.43 us -> none
    pallas_call x0 -> x1, Pallas kernels: none -> 1.69 us  [per_device(): pl.pallas_call(writer, out_shape=(jax.ShapeDtypeStruct((DOCS, 1024), F32)...]
where the time goes in v2:
time: 57.7 us; the launch traced here: 57.6 us
  Pallas kernels  56.8 us (98%)
  between operations  0.8 us (1%)
    pallas_call x1, Pallas kernels, per_device(): pl.pallas_call(body, out_shape=(jax.ShapeDtypeStruct((DOCS, 1024), F32),...  55.1 us
    pallas_call x1, Pallas kernels, per_device(): pl.pallas_call(writer, out_shape=(jax.ShapeDtypeStruct((DOCS, 1024), F32)...  1.69 us

profile of v2, /device:TPU:2, one launch (start us, length us, event | category | flops | bytes accessed | tf_op | source)
XLA Modules:
  0.0 57.6 jit_solution(17217619855292174525)
XLA Ops:
  0.6 55.1 %attn.1 = (f32[4,1024]{1,0:T(4,128)S(1)}, bf16[2048,512]{1,0:T(8,128)(2,1)S(1)}, f32[256,1024]{1,0:T(8,128)S(1)}) custom-call(bf16[2048,512]{1,0:T(8,128)(2,1)} %bitcast.2, bf16[256,512]{1,0:T(8,128)(2,1)} %q_hbm.1, bf16[256,512]{1,0:T(8,128)(2,1)} %c_hbm.1, s32[4]{0:T(128)} %len_hbm.1, s32[4,1024]{1,0:T(4,128)} %beam_hbm.1, f32[4,1024]{1,0:T(4,128)} %grad_hbm.1), custom_call_target="tpu_custom_call" | custom-call | tf_op jit(solution)/shard_map/attn/pallas_call | solution.py:308
  55.7 1.7 %writer.1 = (f32[4,1024]{1,0:T(4,128)}, bf16[2048,512]{1,0:T(8,128)(2,1)}, f32[256,1024]{1,0:T(8,128)}) custom-call(f32[4,1024]{1,0:T(4,128)S(1)} %get-tuple-element.9.a, bf16[2048,512]{1,0:T(8,128)(2,1)S(1)} %get-tuple-element.10.b, f32[256,1024]{1,0:T(8,128)S(1)} %get-tuple-element.11.c), custom_call_target="tpu_custom_call" | custom-call | tf_op jit(solution)/shard_map/writer/pallas_call | solution.py:358

commit v3 on v2

--- a/solution.py
+++ b/solution.py
@@ -85,11 +85,13 @@
     pl.semaphore_wait(barrier, len(greet))
 
     to_partner = [go(remote(W.at[p], W.at[2 + p], gs.at[p], gr.at[p], partner)) for p in range(2)]
-    quarter = pl.ds(pl.multiple_of(y * 64, 64), 64)
+    quarter = pl.ds(pl.multiple_of(y * 48, 16), 48)
     to_across1 = go(remote(W.at[1, quarter], W.at[7, quarter], gs.at[2], gr.at[2], across))
     to_across0 = go(remote(W.at[0], W.at[5], gs.at[3], gr.at[3], across))
+    rest = pl.ds(192, 64)
+    to_across2 = go(remote(W.at[1, rest], W.at[7, rest], gs.at[9], gr.at[9], across))
     to_ring = [
-        remote(W.at[7, quarter], W.at[7, quarter], gs.at[5 + k], gr.at[5 + k], ynb(k)) for k in range(1, 4)
+        remote(W.at[7, quarter], W.at[7, quarter], gs.at[5 + k], gr.at[5 + k], ynb(k)) for k in (2, 1, 3)
     ]
     to_fwd = [remote(W.at[5 + 2 * p], W.at[4 + 2 * p], gs.at[4 + p], gr.at[4 + p], partner) for p in range(2)]
 
@@ -108,7 +110,7 @@
 
     row = lax.broadcasted_iota(jnp.int32, (L, HB), 0)
 
-    def pair(k):
+    def pair(k, last=False):
         ats = [pl.ds(pl.multiple_of(starts[k + i], HB), HB) for i in range(2)]
         w = W[pl.ds(k, 2)].reshape(512, E)
         g = [[G[pl.ds(d, 1), at] for at in ats] for d in range(DOCS)]
@@ -141,6 +143,11 @@
         soft(0)
         scores(2)
         soft(1)
+        if last:
+            scores(3)
+            soft(2)
+            soft(3)
+            return None
         out = lab(0)
         scores(3)
         soft(2)
@@ -179,6 +186,27 @@
             for k in range(1, 4)
         ]
 
+    def last_sends():
+        places = {k: pl.ds(pl.multiple_of(((y + k) % 4) * 128, 128), 128) for k in range(4)}
+        die, cps = {}, []
+        for ks in ((2, 1), (3, 0)):
+            lhs = jnp.concatenate([ST[places[k], :] for k in ks], axis=0)
+            out = jnp.dot(lhs, GA[:, pl.ds(6 * 256, 512)], preferred_element_type=F32)
+            for n, k in enumerate(ks):
+                dsend[3, places[k], :] = out[n * 128 : (n + 1) * 128, :256].astype(BF16)
+                acc[3, places[k], :] = out[n * 128 : (n + 1) * 128, 256:]
+                die[k] = go(remote(dsend.at[3, places[k]], drecv.at[3, places[k]], ds.at[3 + k], dr.at[3 + k], partner))
+        for k in (2, 1, 3, 0):
+            yp = (y + k) % 4
+            die[k].wait_recv()
+            total = acc[3, places[k], :] + drecv[3, places[k], :].astype(F32)
+            if k:
+                ysend[3, yp] = total.astype(BF16)
+                cps.append(go(remote(ysend.at[3, yp], yrecv.at[3, k - 1], ys.at[3, k - 1], yr.at[3, k - 1], ynb(k))))
+            else:
+                yown[3, yp] = total
+        return cps
+
     def y_sum(j, cps):
         for cp in cps:
             cp.wait_recv()
@@ -258,24 +286,22 @@
     d1 = die_send(1, out[:, 256:])
     lax.fori_loop(0, 4, state_grad(True), 0)
     y0 = y_send(0, d0, acc[0])
-    lax.fori_loop(4, 8, state_grad(True), 0)
+    y1 = y_send(1, d1, acc[1])
     to_across0.wait_recv()
     go(to_fwd[0])
-    for cp in to_ring:
+    for cp in to_ring + [to_across2]:
         cp.wait_recv()
     go(to_fwd[1])
-    y1 = y_send(1, d1, acc[1])
     to_fwd[0].wait_recv()
     out = pair(4)
     d2 = die_send(2, out[:, :256])
     acc[2] = out[:, 256:]
+    lax.fori_loop(4, 8, state_grad(True), 0)
     to_fwd[1].wait_recv()
     y2 = y_send(2, d2, acc[2])
-    out = pair(6)
-    d3 = die_send(3, out[:, :256])
-    acc[3] = out[:, 256:]
+    pair(6, True)
+    y3 = last_sends()
     xa0 = x_send_home(0, y0)
-    y3 = y_send(3, d3, acc[3])
     xa1 = x_send_home(1, y1)
     xb0 = x_send_away(0, y2)
     lax.fori_loop(0, 6, state_grad(False), 0)
@@ -339,8 +365,8 @@
             pltpu.VMEM((2, 8, 16, 128), F32),
             pltpu.VMEM((2, 8, 8, 16, 128), BF16),
             dma((11,)),
-            dma((9,)), dma((9,)),
-            dma((4,)), dma((4,)),
+            dma((10,)), dma((10,)),
+            dma((7,)), dma((7,)),
             dma((4, 3)), dma((4, 3)),
             dma((2, 3)), dma((2, 3)),
             dma((2, 7)), dma((2, 7)),

time: 57.7 us -> 57.3 us (level)
  no operation moved by 1% of the time
where the time goes in v3:
time: 57.3 us; the launch traced here: 57.2 us
  Pallas kernels  56.4 us (98%)
  between operations  0.8 us (1%)
    pallas_call x1, Pallas kernels, per_device(): pl.pallas_call(body, out_shape=(jax.ShapeDtypeStruct((DOCS, 1024), F32),...  54.7 us
    pallas_call x1, Pallas kernels, per_device(): pl.pallas_call(writer, out_shape=(jax.ShapeDtypeStruct((DOCS, 1024), F32)...  1.69 us

profile of v3, /device:TPU:2, one launch (start us, length us, event | category | flops | bytes accessed | tf_op | source)
XLA Modules:
  0.0 57.2 jit_solution(16223049844107940230)
XLA Ops:
  0.6 54.7 %attn.1 = (f32[4,1024]{1,0:T(4,128)S(1)}, bf16[2048,512]{1,0:T(8,128)(2,1)S(1)}, f32[256,1024]{1,0:T(8,128)S(1)}) custom-call(bf16[2048,512]{1,0:T(8,128)(2,1)} %bitcast.2, bf16[256,512]{1,0:T(8,128)(2,1)} %q_hbm.1, bf16[256,512]{1,0:T(8,128)(2,1)} %c_hbm.1, s32[4]{0:T(128)} %len_hbm.1, s32[4,1024]{1,0:T(4,128)} %beam_hbm.1, f32[4,1024]{1,0:T(4,128)} %grad_hbm.1), custom_call_target="tpu_custom_call" | custom-call | tf_op jit(solution)/shard_map/attn/pallas_call | solution.py:334
  55.4 1.7 %writer.1 = (f32[4,1024]{1,0:T(4,128)}, bf16[2048,512]{1,0:T(8,128)(2,1)}, f32[256,1024]{1,0:T(8,128)}) custom-call(f32[4,1024]{1,0:T(4,128)S(1)} %get-tuple-element.9.a, bf16[2048,512]{1,0:T(8,128)(2,1)S(1)} %get-tuple-element.10.b, f32[256,1024]{1,0:T(8,128)S(1)} %get-tuple-element.11.c), custom_call_target="tpu_custom_call" | custom-call | tf_op jit(solution)/shard_map/writer/pallas_call | solution.py:384
